TPU v7x, 32 devices: a whole 2x2x4 slice. The times are simulated.
32 devices in a mesh: dp: 8 (over y, x, core), group: 4 (over z).
Axes of the slice: x: 2, y: 2, z: 4, core: 2. Of those that a mesh axis runs over, the one named last changes fastest.
Arguments:
- inputs: float32 [4096, 768], P(('dp', 'group')), may hold values from -6 to 6
- cotangent: float32 [4096, 768], P(('dp', 'group')), may hold values from -6 to 6
- lengths: int32 [32, 4], P(('dp', 'group')), may hold values from 1 to 64, 128 in all within a row
- attn_weights: float32 [4, 768, 768], P('group', 'dp'), may hold values from -1 to 1
- attn_momenta: float32 [4, 768, 768], P('group', 'dp'), may hold values from -1 to 1
- ffn_weights: float32 [2, 768, 3072], P(None, 'dp', 'group'), may hold values from -1 to 1
- ffn_momenta: float32 [2, 768, 3072], P(None, 'dp', 'group'), may hold values from -1 to 1
- vectors: float32 [12, 768], replicated, may hold values from -2 to 2
- vector_momenta: float32 [12, 768], replicated, may hold values from -1 to 1
Outputs:
- outputs: float32 [4096, 768], P(('dp', 'group'))
- input_grad: float32 [4096, 768], P(('dp', 'group'))
- attn_grads: float32 [4, 768, 768], P('group', 'dp')
- ffn_grads: float32 [2, 768, 3072], P(None, 'dp', 'group')
- vector_grads: float32 [12, 768], replicated
- new_attn_weights: float32 [4, 768, 768], P('group', 'dp')
- new_attn_momenta: float32 [4, 768, 768], P('group', 'dp')
- new_ffn_weights: float32 [2, 768, 3072], P(None, 'dp', 'group')
- new_ffn_momenta: float32 [2, 768, 3072], P(None, 'dp', 'group')
- new_vectors: float32 [12, 768], replicated
- new_vector_momenta: float32 [12, 768], replicated
Inputs may be any that keep to these rules, and one draw needn't show every extreme that they name: Each device's 4 lengths sum to 128.
All inputs are finite; a program needn't handle non-finite values.
Results may differ from a plain program's by a relative error of at most 0.025.
The roundings to bfloat16 on the way count: a program that leaves them out, or rounds other values in their place, can miss the bound.
Values may be sent and summed in bfloat16 or wider, within the bound.
A program may use at most 128 MiB of HBM per device.

v0:
```python
import math
import jax
import jax.numpy as jnp
from jax import lax
from jax.sharding import PartitionSpec as P

HEADS = 12
NS_ITERS = 3
coef_first = 3.4445
coef_second = -4.775
coef_third = 2.0315
momentum_rate = 0.9
muon_rate = 0.8
vector_rate = 0.1


def norm_forward(rows):
    centre = jnp.mean(rows, axis=1, keepdims=True)
    centred = rows - centre
    variance = jnp.mean(centred * centred, axis=1, keepdims=True)
    inverse = lax.rsqrt(variance + 1e-05)
    return (centred * inverse, inverse)


def norm_backward(grad_normed, normed, inverse):
    return inverse * (
        grad_normed
        - jnp.mean(grad_normed, axis=1, keepdims=True)
        - normed * jnp.mean(grad_normed * normed, axis=1, keepdims=True)
    )


def masked_scores(query_heads, key_heads, allowed):
    scores = jnp.einsum("qhd,khd->hqk", query_heads, key_heads, preferred_element_type=jnp.float32)
    return jnp.where(allowed[None], scores, -jnp.inf)


def layer_block(block_rows, block_cotan, seq_lengths, attn_w, ffn_w, vectors):
    token_count = block_rows.shape[0]
    width = block_rows.shape[1]
    head_size = width // HEADS
    scale = 1.0 / math.sqrt(head_size)
    w_query, w_key, w_value, w_output = (attn_w[0], attn_w[1], attn_w[2], attn_w[3])
    w_expand, w_reduce = (ffn_w[0], ffn_w[1])
    expand_bias = vectors[8:].reshape(-1)
    positions = jnp.arange(token_count, dtype=jnp.int32)
    seq_ends = jnp.cumsum(seq_lengths)
    segment = jnp.sum((positions[:, None] >= seq_ends[None, :]).astype(jnp.int32), axis=1)
    allowed = (segment[:, None] == segment[None, :]) & (positions[None, :] <= positions[:, None])
    normed_first, inverse_first = norm_forward(block_rows)
    hidden_first = (normed_first * vectors[0] + vectors[1]).astype(jnp.bfloat16)
    query = (
        (jnp.dot(hidden_first, w_query, preferred_element_type=jnp.float32) + vectors[2]) * scale
    ).astype(jnp.bfloat16)
    keyed = jnp.dot(hidden_first, w_key, preferred_element_type=jnp.float32).astype(jnp.bfloat16)
    valued = (
        jnp.dot(hidden_first, w_value, preferred_element_type=jnp.float32) + vectors[3]
    ).astype(jnp.bfloat16)
    query_heads = query.reshape(token_count, HEADS, head_size)
    key_heads = keyed.reshape(token_count, HEADS, head_size)
    value_heads = valued.reshape(token_count, HEADS, head_size)
    scores = masked_scores(query_heads, key_heads, allowed)
    highest = jnp.max(scores, axis=2, keepdims=True)
    log_total = highest + jnp.log(jnp.sum(jnp.exp(scores - highest), axis=2, keepdims=True))
    probs_first = jnp.exp(scores - log_total).astype(jnp.bfloat16)
    attended = jnp.einsum(
        "hqk,khd->qhd", probs_first, value_heads, preferred_element_type=jnp.float32
    )
    attended = attended.reshape(token_count, width).astype(jnp.bfloat16)
    middle = (
        block_rows + jnp.dot(attended, w_output, preferred_element_type=jnp.float32) + vectors[4]
    )
    normed_second, inverse_second = norm_forward(middle)
    hidden_second = (normed_second * vectors[5] + vectors[6]).astype(jnp.bfloat16)
    before = jnp.dot(hidden_second, w_expand, preferred_element_type=jnp.float32) + expand_bias
    active = jnp.maximum(before, 0.0).astype(jnp.bfloat16)
    outputs = (
        middle
        + jnp.einsum("tf,df->td", active, w_reduce, preferred_element_type=jnp.float32)
        + vectors[7]
    )
    cotan_b = block_cotan.astype(jnp.bfloat16)
    grad_active = jnp.dot(cotan_b, w_reduce, preferred_element_type=jnp.float32)
    grad_before = jnp.where(before > 0.0, grad_active, 0.0)
    before_grad_b = grad_before.astype(jnp.bfloat16)
    grad_second = jnp.einsum(
        "tf,cf->tc", before_grad_b, w_expand, preferred_element_type=jnp.float32
    )
    grad_middle = block_cotan + norm_backward(
        grad_second * vectors[5], normed_second, inverse_second
    )
    middle_b = grad_middle.astype(jnp.bfloat16)
    grad_attended = jnp.einsum(
        "td,cd->tc", middle_b, w_output, preferred_element_type=jnp.float32
    ).astype(jnp.bfloat16)
    attended_heads = grad_attended.reshape(token_count, HEADS, head_size)
    probs = jnp.exp(masked_scores(query_heads, key_heads, allowed) - log_total)
    probs_b = probs.astype(jnp.bfloat16)
    grad_probs = jnp.einsum(
        "qhd,khd->hqk", attended_heads, value_heads, preferred_element_type=jnp.float32
    )
    grad_value = jnp.einsum(
        "hqk,qhd->khd", probs_b, attended_heads, preferred_element_type=jnp.float32
    )
    delta = jnp.sum(probs * grad_probs, axis=2, keepdims=True)
    grad_scores = (probs * (grad_probs - delta)).astype(jnp.bfloat16)
    grad_query = (
        jnp.einsum("hqk,khd->qhd", grad_scores, key_heads, preferred_element_type=jnp.float32)
        * scale
    )
    grad_key = jnp.einsum(
        "hqk,qhd->khd", grad_scores, query_heads, preferred_element_type=jnp.float32
    )
    query_grad = grad_query.reshape(token_count, width)
    key_grad = grad_key.reshape(token_count, width)
    value_grad = grad_value.reshape(token_count, width)
    query_grad_b = query_grad.astype(jnp.bfloat16)
    key_grad_b = key_grad.astype(jnp.bfloat16)
    value_grad_b = value_grad.astype(jnp.bfloat16)
    grad_first = jnp.einsum("td,cd->tc", query_grad_b, w_query, preferred_element_type=jnp.float32)
    grad_first = grad_first + jnp.einsum(
        "td,cd->tc", key_grad_b, w_key, preferred_element_type=jnp.float32
    )
    grad_first = grad_first + jnp.einsum(
        "td,cd->tc", value_grad_b, w_value, preferred_element_type=jnp.float32
    )
    input_grad = grad_middle + norm_backward(grad_first * vectors[0], normed_first, inverse_first)
    small_terms = jnp.stack(
        [
            jnp.sum(grad_first * normed_first, axis=0),
            jnp.sum(grad_first, axis=0),
            jnp.sum(query_grad, axis=0),
            jnp.sum(value_grad, axis=0),
            jnp.sum(grad_middle, axis=0),
            jnp.sum(grad_second * normed_second, axis=0),
            jnp.sum(grad_second, axis=0),
            jnp.sum(block_cotan, axis=0),
        ]
    )
    bias_terms = jnp.sum(grad_before, axis=0).reshape(-1, width)
    vector_terms = jnp.concatenate([small_terms, bias_terms], axis=0)
    pieces = (
        hidden_first,
        attended,
        query_grad_b,
        key_grad_b,
        value_grad_b,
        middle_b,
        hidden_second,
        cotan_b,
        before_grad_b,
        active,
    )
    return (outputs, input_grad, vector_terms, pieces)


def owned_terms(pieces):
    group_count = lax.axis_size("group")
    own_index = lax.axis_index("group")
    (
        hidden_first,
        attended,
        query_grad_b,
        key_grad_b,
        value_grad_b,
        middle_b,
        hidden_second,
        cotan_b,
        before_grad_b,
        active,
    ) = pieces
    quarter = before_grad_b.shape[1] // group_count
    gathered = (
        lax.all_gather(hidden_first, "group", axis=0, tiled=True),
        lax.all_gather(attended, "group", axis=0, tiled=True),
        lax.all_gather(query_grad_b, "group", axis=0, tiled=True),
        lax.all_gather(key_grad_b, "group", axis=0, tiled=True),
        lax.all_gather(value_grad_b, "group", axis=0, tiled=True),
        lax.all_gather(middle_b, "group", axis=0, tiled=True),
        lax.all_gather(hidden_second, "group", axis=0, tiled=True),
        lax.all_gather(cotan_b, "group", axis=0, tiled=True),
        lax.all_gather(before_grad_b, "group", axis=0, tiled=True),
        lax.all_gather(active, "group", axis=0, tiled=True),
    )
    (
        all_first,
        all_attended,
        all_query,
        all_key,
        all_value,
        all_middle,
        all_second,
        all_cotan,
        all_before,
        all_active,
    ) = gathered
    left_side = jnp.where(own_index == 3, all_attended, all_first)
    right_stack = jnp.stack([all_query, all_key, all_value, all_middle])
    right_side = lax.dynamic_index_in_dim(right_stack, own_index, 0, keepdims=False)
    before_part = lax.dynamic_slice_in_dim(all_before, own_index * quarter, quarter, 1)
    active_part = lax.dynamic_slice_in_dim(all_active, own_index * quarter, quarter, 1)
    attn_term = jnp.einsum("tc,td->cd", left_side, right_side, preferred_element_type=jnp.float32)
    ffn_term = jnp.stack(
        [
            jnp.einsum("tc,tf->cf", all_second, before_part, preferred_element_type=jnp.float32),
            jnp.einsum("td,tf->df", all_cotan, active_part, preferred_element_type=jnp.float32),
        ]
    )
    return (attn_term, ffn_term)


def orthogonalize_rows(attn_rows, ffn_rows, attn_square, ffn_square):
    attn_iter = attn_rows / (jnp.sqrt(attn_square) + 1e-07)
    ffn_iter = ffn_rows / (jnp.sqrt(ffn_square)[:, None, None] + 1e-07)
    for iteration in range(NS_ITERS):
        attn_iter_b = attn_iter.astype(jnp.bfloat16)
        ffn_iter_b = ffn_iter.astype(jnp.bfloat16)
        attn_full, ffn_full = (
            lax.all_gather(attn_iter_b, "dp", axis=0, tiled=True),
            lax.all_gather(ffn_iter_b, "dp", axis=1, tiled=True),
        )
        attn_gram = jnp.einsum(
            "ik,jk->ij", attn_iter_b, attn_full, preferred_element_type=jnp.float32
        )
        ffn_part = jnp.einsum(
            "mik,mjk->mij", ffn_iter_b, ffn_full, preferred_element_type=jnp.float32
        )
        ffn_gram = lax.psum(ffn_part, "group")
        attn_gram_b = attn_gram.astype(jnp.bfloat16)
        ffn_gram_b = ffn_gram.astype(jnp.bfloat16)
        attn_gram_full, ffn_gram_full = (
            lax.all_gather(attn_gram_b, "dp", axis=0, tiled=True),
            lax.all_gather(ffn_gram_b, "dp", axis=1, tiled=True),
        )
        attn_mixed = coef_second * attn_gram + coef_third * jnp.dot(
            attn_gram_b, attn_gram_full, preferred_element_type=jnp.float32
        )
        ffn_mixed = coef_second * ffn_gram + coef_third * jnp.einsum(
            "mik,mkj->mij", ffn_gram_b, ffn_gram_full, preferred_element_type=jnp.float32
        )
        attn_iter = coef_first * attn_iter + jnp.dot(
            attn_mixed.astype(jnp.bfloat16), attn_full, preferred_element_type=jnp.float32
        )
        ffn_iter = coef_first * ffn_iter + jnp.einsum(
            "mik,mkj->mij",
            ffn_mixed.astype(jnp.bfloat16),
            ffn_full,
            preferred_element_type=jnp.float32,
        )
    return (attn_iter, ffn_iter)


def on_device(
    inputs,
    cotangent,
    lengths,
    attn_weights,
    attn_momenta,
    ffn_weights,
    ffn_momenta,
    vectors,
    vector_momenta,
):
    own_attn = attn_weights.astype(jnp.bfloat16)
    own_ffn = ffn_weights.astype(jnp.bfloat16)
    attn_rows, ffn_rows = (
        lax.all_gather(own_attn, "dp", axis=1, tiled=True),
        lax.all_gather(own_ffn, "dp", axis=1, tiled=True),
    )
    attn_whole, ffn_whole = (
        lax.all_gather(attn_rows, "group", axis=0, tiled=True),
        lax.all_gather(ffn_rows, "group", axis=2, tiled=True),
    )
    outputs, input_grad, vector_terms, pieces = layer_block(
        inputs, cotangent, lengths[0], attn_whole, ffn_whole, vectors
    )
    attn_term, ffn_term = owned_terms(pieces)
    attn_total, ffn_total = (
        lax.psum_scatter(attn_term, "dp", scatter_dimension=0, tiled=True),
        lax.psum_scatter(ffn_term, "dp", scatter_dimension=1, tiled=True),
    )
    group_count = lax.axis_size("group")
    total_tokens = float(inputs.shape[0] * lax.axis_size("dp") * group_count)
    attn_grads = attn_total[None] / total_tokens
    ffn_grads = ffn_total / total_tokens
    attn_next = momentum_rate * attn_momenta + attn_grads
    ffn_next = momentum_rate * ffn_momenta + ffn_grads
    owner_mask = (jnp.arange(group_count, dtype=jnp.int32) == lax.axis_index("group")).astype(
        jnp.float32
    )
    square_terms = jnp.concatenate(
        [owner_mask * jnp.sum(attn_next * attn_next), jnp.sum(ffn_next * ffn_next, axis=(1, 2))]
    )
    vector_total, square_total = lax.psum((vector_terms, square_terms), ("dp", "group"))
    attn_square = jnp.sum(square_total[:group_count] * owner_mask)
    ffn_square = square_total[group_count:]
    attn_step, ffn_step = orthogonalize_rows(attn_next[0], ffn_next, attn_square, ffn_square)
    new_attn_weights = attn_weights - muon_rate * attn_step[None]
    new_ffn_weights = ffn_weights - muon_rate * ffn_step
    vector_grads = vector_total / total_tokens
    new_vector_momenta = momentum_rate * vector_momenta + vector_grads
    spread = lax.rsqrt(
        jnp.mean(new_vector_momenta * new_vector_momenta, axis=1, keepdims=True) + 1e-06
    )
    new_vectors = vectors - vector_rate * new_vector_momenta * spread
    return (
        outputs,
        input_grad,
        attn_grads,
        ffn_grads,
        vector_grads,
        new_attn_weights,
        attn_next,
        new_ffn_weights,
        ffn_next,
        new_vectors,
        new_vector_momenta,
    )


def solution(mesh):
    in_specs = (
        P(("dp", "group"), None),
        P(("dp", "group"), None),
        P(("dp", "group"), None),
        P("group", "dp", None),
        P("group", "dp", None),
        P(None, "dp", "group"),
        P(None, "dp", "group"),
        P(),
        P(),
    )
    out_specs = (
        P(("dp", "group"), None),
        P(("dp", "group"), None),
        P("group", "dp", None),
        P(None, "dp", "group"),
        P(),
        P("group", "dp", None),
        P("group", "dp", None),
        P(None, "dp", "group"),
        P(None, "dp", "group"),
        P(),
        P(),
    )
    return jax.shard_map(
        on_device, mesh=mesh, in_specs=in_specs, out_specs=out_specs, check_vma=False
    )
```

profile of v0, /device:TPU:0, one launch (start us, length us, event | category | flops | bytes accessed | tf_op | source)
XLA Modules:
  0.0 1140.3 jit_solution(3156177068706588488)
XLA Ops:
  10.9 26.2 %all-gather.20.cloned.1.call-done = bf16[1,768,768]{2,1,0:T(8,128)(2,1)} async-done(((bf16[1,96,768]{2,1,0:T(8,128)(2,1)}), bf16[1,768,768]{2,1,0:T(8,128)(2,1)}) %all-gather.20.cloned.1.call-update) | async-done | bytes 1179664 | tf_op jit(solution)/shard_map/all_gather | solution.py:267
  37.2 31.3 %all-gather.24.cloned.1.call-done = bf16[2,768,768]{2,1,0:T(8,128)(2,1)} async-done(((bf16[2,96,768]{2,1,0:T(8,128)(2,1)}), bf16[2,768,768]{2,1,0:T(8,128)(2,1)}) %all-gather.24.cloned.1.call-update) | async-done | bytes 2359312 | tf_op jit(solution)/shard_map/all_gather | solution.py:268
  70.1 89.4 %all-gather.22.cloned.1.call-done = bf16[4,768,768]{2,1,0:T(8,128)(2,1)} async-done(((bf16[1,768,768]{2,1,0:T(8,128)(2,1)}), bf16[4,768,768]{2,1,0:T(8,128)(2,1)}) %all-gather.22.cloned.1.call-update) | async-done | bytes 4718608 | tf_op jit(solution)/shard_map/all_gather | solution.py:271
  167.8 158.3 %all-gather.26.cloned.1.call-done = bf16[2,768,3072]{2,1,0:T(8,128)(2,1)} async-done(((bf16[2,768,768]{2,1,0:T(8,128)(2,1)}), bf16[2,768,3072]{2,1,0:T(8,128)(2,1)}) %all-gather.26.cloned.1.call-update) | async-done | bytes 9437200 | tf_op jit(solution)/shard_map/all_gather | solution.py:272
  326.1 4.6 maximum_convert_fusion
  331.4 5.2 fusion.91
  336.7 31.7 %all_gather.83 = bf16[512,768]{1,0:T(8,128)(2,1)} all-gather(bf16[128,768]{1,0:T(8,128)(2,1)S(1)} %add_convert_fusion.1), channel_id=1, replica_groups=mesh['dp'=8,'group'=4] {'group'}, dimensions={0}, use_global_device_ids=true | all-gather | bytes 983040 | tf_op jit(solution)/shard_map/all_gather | solution.py:174
  368.5 30.0 %all_gather.82 = bf16[512,768]{1,0:T(8,128)(2,1)} all-gather(bf16[128,768]{1,0:T(8,128)(2,1)S(1)} %copy.71), channel_id=1, replica_groups=mesh['dp'=8,'group'=4] {'group'}, dimensions={0}, use_global_device_ids=true | all-gather | bytes 983040 | tf_op jit(solution)/shard_map/all_gather | solution.py:175
  398.5 5.0 multiply_reduce_fusion.2
  413.3 18.2 %all_gather.87 = bf16[512,768]{1,0:T(8,128)(2,1)S(1)} all-gather(bf16[128,768]{1,0:T(8,128)(2,1)} %copy-done.31), channel_id=1, replica_groups=mesh['dp'=8,'group'=4] {'group'}, dimensions={0}, use_global_device_ids=true | all-gather | bytes 983040 | tf_op jit(solution)/shard_map/all_gather | solution.py:179
  431.6 29.5 %all_gather.84 = bf16[512,768]{1,0:T(8,128)(2,1)S(1)} all-gather(bf16[128,768]{1,0:T(8,128)(2,1)S(1)} %copy-done.25), channel_id=1, replica_groups=mesh['dp'=8,'group'=4] {'group'}, dimensions={0}, use_global_device_ids=true | all-gather | bytes 983040 | tf_op jit(solution)/shard_map/all_gather | solution.py:176
  461.1 29.8 %all_gather.85 = bf16[512,768]{1,0:T(8,128)(2,1)S(1)} all-gather(bf16[128,768]{1,0:T(8,128)(2,1)} %copy.73), channel_id=1, replica_groups=mesh['dp'=8,'group'=4] {'group'}, dimensions={0}, use_global_device_ids=true | all-gather | bytes 983040 | tf_op jit(solution)/shard_map/all_gather | solution.py:177
  491.0 28.4 %all_gather.86 = bf16[512,768]{1,0:T(8,128)(2,1)S(1)} all-gather(bf16[128,768]{1,0:T(8,128)(2,1)S(1)} %copy-done.26), channel_id=1, replica_groups=mesh['dp'=8,'group'=4] {'group'}, dimensions={0}, use_global_device_ids=true | all-gather | bytes 983040 | tf_op jit(solution)/shard_map/all_gather | solution.py:178
  519.4 2.5 fusion.42
  522.8 17.2 %all_gather.91 = bf16[512,768]{1,0:T(8,128)(2,1)} all-gather(bf16[128,768]{1,0:T(8,128)(2,1)S(1)} %copy-done.30), channel_id=1, replica_groups=mesh['dp'=8,'group'=4] {'group'}, dimensions={0}, use_global_device_ids=true | all-gather | bytes 983040 | tf_op jit(solution)/shard_map/all_gather | solution.py:181
  540.0 16.6 %all_gather.88 = bf16[512,768]{1,0:T(8,128)(2,1)} all-gather(bf16[128,768]{1,0:T(8,128)(2,1)S(1)} %copy-done.28), channel_id=1, replica_groups=mesh['dp'=8,'group'=4] {'group'}, dimensions={0}, use_global_device_ids=true | all-gather | bytes 983040 | tf_op jit(solution)/shard_map/all_gather | solution.py:180
  561.1 2.4 pad_maximum_fusion
  568.3 3.2 multiply_reduce_fusion.3
  574.9 46.3 %reduce-scatter.5.cloned.1.call-done = f32[2,96,768]{2,1,0:T(8,128)} async-done(((f32[2,768,768]{2,1,0:T(8,128)}), f32[2,96,768]{2,1,0:T(8,128)}) %reduce-scatter.5.cloned.1.call-update) | async-done | bytes 589840 | tf_op jit(solution)/shard_map/reduce_scatter | solution.py:280
  623.3 40.2 %all-reduce = (f32[12,768]{1,0:T(8,128)}, f32[6]{0:T(128)S(1)}) all-reduce(f32[12,768]{1,0:T(8,128)S(1)} %concatenate.6, f32[6]{0:T(128)S(1)} %pad_maximum_fusion.1), channel_id=1, replica_groups=mesh['dp'=8,'group'=4] {'dp','group'}, use_global_device_ids=true, to_apply=%region_24.25 | all-reduce | flops 9222 | bytes 73776 | tf_op jit(solution)/shard_map/psum | solution.py:294
  664.5 29.7 %all-gather.42.cloned.1.call-done = bf16[2,768,768]{2,1,0:T(8,128)(2,1)} async-done(((bf16[2,96,768]{2,1,0:T(8,128)(2,1)}), bf16[2,768,768]{2,1,0:T(8,128)(2,1)}) %all-gather.42.cloned.1.call-update) | async-done | bytes 2359312 | tf_op jit(solution)/shard_map/all_gather | solution.py:220
  694.2 3.6 fusion.110
  697.8 39.8 %all-reduce.5.cloned.1.call-done = f32[2,96,768]{2,1,0:T(8,128)} async-done(((f32[2,96,768]{2,1,0:T(8,128)}), f32[2,96,768]{2,1,0:T(8,128)}) %all-reduce.5.cloned.1.call-update) | async-done | bytes 589840 | tf_op jit(solution)/shard_map/psum | solution.py:228
  742.5 26.0 %all-gather.44.cloned.1.call-done = bf16[2,768,768]{2,1,0:T(8,128)(2,1)} async-done(((bf16[2,96,768]{2,1,0:T(8,128)(2,1)}), bf16[2,768,768]{2,1,0:T(8,128)(2,1)}) %all-gather.44.cloned.1.call-update) | async-done | bytes 2359312 | tf_op jit(solution)/shard_map/all_gather | solution.py:233
  768.5 4.0 fusion.102
  772.5 22.2 %all-gather.54.cloned.1.call-done = bf16[1,768,768]{2,1,0:T(8,128)(2,1)} async-done(((bf16[1,96,768]{2,1,0:T(8,128)(2,1)}), bf16[1,768,768]{2,1,0:T(8,128)(2,1)}) %all-gather.54.cloned.1.call-update) | async-done | bytes 1179664 | tf_op jit(solution)/shard_map/all_gather | solution.py:219
  794.7 2.5 fusion.97
  797.3 28.8 %all-gather.46.cloned.1.call-done = bf16[2,768,768]{2,1,0:T(8,128)(2,1)} async-done(((bf16[2,96,768]{2,1,0:T(8,128)(2,1)}), bf16[2,768,768]{2,1,0:T(8,128)(2,1)}) %all-gather.46.cloned.1.call-update) | async-done | bytes 2359312 | tf_op jit(solution)/shard_map/all_gather | solution.py:220
  826.1 3.3 fusion.111
  829.5 22.3 %all-gather.32.cloned.1.call-done = bf16[768,768]{1,0:T(8,128)(2,1)} async-done(((bf16[96,768]{1,0:T(8,128)(2,1)}), bf16[768,768]{1,0:T(8,128)(2,1)}) %all-gather.32.cloned.1.call-update) | async-done | bytes 1179664 | tf_op jit(solution)/shard_map/all_gather | solution.py:232
  851.8 2.6 fusion.98
  854.5 39.2 %all-reduce.7.cloned.1.call-done = f32[2,96,768]{2,1,0:T(8,128)} async-done(((f32[2,96,768]{2,1,0:T(8,128)}), f32[2,96,768]{2,1,0:T(8,128)}) %all-reduce.7.cloned.1.call-update) | async-done | bytes 589840 | tf_op jit(solution)/shard_map/psum | solution.py:228
  895.5 23.3 %all-gather.34.cloned.1.call-done = bf16[768,768]{1,0:T(8,128)(2,1)} async-done(((bf16[96,768]{1,0:T(8,128)(2,1)}), bf16[768,768]{1,0:T(8,128)(2,1)}) %all-gather.34.cloned.1.call-update) | async-done | bytes 1179664 | tf_op jit(solution)/shard_map/all_gather | solution.py:219
  918.8 2.6 fusion.99
  921.5 28.0 %all-gather.48.cloned.1.call-done = bf16[2,768,768]{2,1,0:T(8,128)(2,1)} async-done(((bf16[2,96,768]{2,1,0:T(8,128)(2,1)}), bf16[2,768,768]{2,1,0:T(8,128)(2,1)}) %all-gather.48.cloned.1.call-update) | async-done | bytes 2359312 | tf_op jit(solution)/shard_map/all_gather | solution.py:233
  949.5 3.9 fusion.103
  953.5 21.7 %all-gather.36.cloned.1.call-done = bf16[768,768]{1,0:T(8,128)(2,1)} async-done(((bf16[96,768]{1,0:T(8,128)(2,1)}), bf16[768,768]{1,0:T(8,128)(2,1)}) %all-gather.36.cloned.1.call-update) | async-done | bytes 1179664 | tf_op jit(solution)/shard_map/all_gather | solution.py:232
  975.2 3.2 fusion.100
  978.4 27.6 %all-gather.50.cloned.1.call-done = bf16[2,768,768]{2,1,0:T(8,128)(2,1)} async-done(((bf16[2,96,768]{2,1,0:T(8,128)(2,1)}), bf16[2,768,768]{2,1,0:T(8,128)(2,1)}) %all-gather.50.cloned.1.call-update) | async-done | bytes 2359312 | tf_op jit(solution)/shard_map/all_gather | solution.py:220
  1006.0 3.3 fusion.112
  1009.5 22.2 %all-gather.38.cloned.1.call-done = bf16[768,768]{1,0:T(8,128)(2,1)} async-done(((bf16[96,768]{1,0:T(8,128)(2,1)}), bf16[768,768]{1,0:T(8,128)(2,1)}) %all-gather.38.cloned.1.call-update) | async-done | bytes 1179664 | tf_op jit(solution)/shard_map/all_gather | solution.py:219
  1031.7 2.5 fusion.101
  1034.5 39.2 %all-reduce.9.cloned.1.call-done = f32[2,96,768]{2,1,0:T(8,128)} async-done(((f32[2,96,768]{2,1,0:T(8,128)}), f32[2,96,768]{2,1,0:T(8,128)}) %all-reduce.9.cloned.1.call-update) | async-done | bytes 589840 | tf_op jit(solution)/shard_map/psum | solution.py:228
  1076.6 4.8 fusion.18
  1082.9 16.1 %all-gather.40.cloned.1.call-done = bf16[768,768]{1,0:T(8,128)(2,1)} async-done(((bf16[96,768]{1,0:T(8,128)(2,1)}), bf16[768,768]{1,0:T(8,128)(2,1)}) %all-gather.40.cloned.1.call-update) | async-done | bytes 1179664 | tf_op jit(solution)/shard_map/all_gather | solution.py:232
  1099.0 3.2 fusion.33
  1102.2 27.6 %all-gather.52.cloned.1.call-done = bf16[2,768,768]{2,1,0:T(8,128)(2,1)} async-done(((bf16[2,96,768]{2,1,0:T(8,128)(2,1)}), bf16[2,768,768]{2,1,0:T(8,128)(2,1)}) %all-gather.52.cloned.1.call-update) | async-done | bytes 2359312 | tf_op jit(solution)/shard_map/all_gather | solution.py:233
  1129.9 3.9 fusion.7
  (244 shorter events, 51.7 us)
Async XLA Ops:
  7.2 29.9 %all-gather.20.cloned.1.call-start = ((), (), s32[]{:S(2)}) async-start(), calls=%async_computation.2 | async-start | bytes 1327104 | tf_op jit(solution)/shard_map/all_gather | solution.py:267
  8.9 59.7 %slice-start = ((f32[12,768]{1,0:T(8,128)}), f32[4,768]{1,0:T(4,128)S(1)}, s32[]{:S(2)}) async-start(f32[12,768]{1,0:T(8,128)} %param.16), calls=%async_computation.25 | async-start | bytes 24576 | tf_op jit(solution)/shard_map/slice | solution.py:45
  8.9 59.7 %copy-start = (f32[128,768]{1,0:T(8,128)S(1)}, f32[128,768]{1,0:T(8,128)}, u32[]{:S(2)}) copy-start(f32[128,768]{1,0:T(8,128)} %param.9) | copy-start | bytes 1179652
  8.9 59.6 %all-gather.24.cloned.1.call-start = ((), (), s32[]{:S(2)}) async-start(), calls=%async_computation.4 | async-start | bytes 2654208 | tf_op jit(solution)/shard_map/all_gather | solution.py:268
  10.8 57.9 %copy-start.55 = (s32[1,4]{1,0:T(1,128)S(1)}, s32[1,4]{1,0:T(1,128)}, u32[]{:S(2)}) copy-start(s32[1,4]{1,0:T(1,128)} %param.11) | copy-start | bytes 52
  10.8 58.2 %copy-start.36 = (f32[12,768]{1,0:T(8,128)S(1)}, f32[12,768]{1,0:T(8,128)}, u32[]{:S(2)}) copy-start(f32[12,768]{1,0:T(8,128)} %param.16) | copy-start | bytes 110596
  10.8 148.7 %all-gather.22.cloned.1.call-start = ((), (), s32[]{:S(2)}) async-start(), calls=%async_computation.3 | async-start | bytes 5898240 | tf_op jit(solution)/shard_map/all_gather | solution.py:271
  37.1 289.0 %all-gather.26.cloned.1.call-start = ((), (), s32[]{:S(2)}) async-start(), calls=%async_computation.5 | async-start | bytes 11796480 | tf_op jit(solution)/shard_map/all_gather | solution.py:272
  68.5 488.0 %all-gather.30.cloned.1.call-start = ((), (), s32[]{:S(2)}) async-start(), calls=%async_computation.8 | async-start | bytes 3932160 | tf_op jit(solution)/shard_map/all_gather | solution.py:183
  69.6 93.2 %copy-start.45 = (f32[128]{0:T(128)}, f32[128]{0:T(128)S(1)}, u32[]{:S(2)}) copy-start(f32[128]{0:T(128)S(1)} %broadcast_multiply_fusion.7) | copy-start | bytes 1540
  69.8 89.7 %copy-start.51 = (f32[128]{0:T(128)}, f32[128]{0:T(128)S(1)}, u32[]{:S(2)}) copy-start(f32[128]{0:T(128)S(1)} %add_rsqrt_fusion.1) | copy-start | bytes 1540
  167.4 231.0 %copy-start.47 = (f32[128]{0:T(128)}, f32[128]{0:T(128)S(1)}, u32[]{:S(2)}) copy-start(f32[128]{0:T(128)S(1)} %broadcast_multiply_fusion.6) | copy-start | bytes 1540
  167.7 230.8 %copy-start.54 = (f32[128]{0:T(128)}, f32[128]{0:T(128)S(1)}, u32[]{:S(2)}) copy-start(f32[128]{0:T(128)S(1)} %add_rsqrt_fusion) | copy-start | bytes 1540
  167.8 162.9 %copy-start.27 = (bf16[128,768]{1,0:T(8,128)(2,1)}, bf16[128,768]{1,0:T(8,128)(2,1)S(1)}, u32[]{:S(2)}) copy-start(bf16[128,768]{1,0:T(8,128)(2,1)S(1)} %add_convert_fusion) | copy-start | bytes 589828
  167.8 163.0 %copy-start.16 = (f32[128,768]{1,0:T(8,128)S(1)}, f32[128,768]{1,0:T(8,128)}, u32[]{:S(2)}) copy-start(f32[128,768]{1,0:T(8,128)} %param.10) | copy-start | bytes 1179652
  330.7 228.2 %all-gather.28.cloned.1.call-start = ((), (), s32[]{:S(2)}) async-start(), calls=%async_computation.7 | async-start | bytes 3932160 | tf_op jit(solution)/shard_map/all_gather | solution.py:182
  336.6 235.2 %reduce-scatter.3.cloned.1.call-start = ((), (), s32[]{:S(2)}) async-start(), calls=%async_computation.6 | async-start | bytes 2654208 | tf_op jit(solution)/shard_map/reduce_scatter | solution.py:279
  410.6 80.4 %copy-start.12 = (bf16[12,64,128]{2,1,0:T(8,128)(2,1)}, bf16[12,64,128]{2,1,0:T(8,128)(2,1)S(1)}, u32[]{:S(2)}) copy-start(bf16[12,64,128]{2,1,0:T(8,128)(2,1)S(1)} %convolution_convert_fusion) | copy-start | bytes 589828
  412.5 109.4 %copy-start.20 = (bf16[128,12,64]{0,2,1:T(8,128)(2,1)}, bf16[128,12,64]{0,2,1:T(8,128)(2,1)S(1)}, u32[]{:S(2)}) copy-start(bf16[128,12,64]{0,2,1:T(8,128)(2,1)S(1)} %get-tuple-element.45) | copy-start | bytes 589828
  412.5 106.9 %copy-start.23 = (bf16[512,768]{1,0:T(8,128)(2,1)S(1)}, bf16[512,768]{1,0:T(8,128)(2,1)}, u32[]{:S(2)}) copy-start(bf16[512,768]{1,0:T(8,128)(2,1)} %all_gather.83) | copy-start | bytes 2359300
  412.5 106.9 %copy-start.24 = (bf16[512,768]{1,0:T(8,128)(2,1)S(1)}, bf16[512,768]{1,0:T(8,128)(2,1)}, u32[]{:S(2)}) copy-start(bf16[512,768]{1,0:T(8,128)(2,1)} %all_gather.82) | copy-start | bytes 2359300
  413.3 77.6 %copy-start.26 = (bf16[128,768]{1,0:T(8,128)(2,1)S(1)}, bf16[128,768]{1,0:T(8,128)(2,1)}, u32[]{:S(2)}) copy-start(bf16[128,768]{1,0:T(8,128)(2,1)} %copy.74) | copy-start | bytes 589828
  521.9 99.3 %reduce-scatter.5.cloned.1.call-start = ((), (), s32[]{:S(2)}) async-start(), calls=%async_computation.9 | async-start | bytes 5308416 | tf_op jit(solution)/shard_map/reduce_scatter | solution.py:280
  563.6 130.6 %all-gather.42.cloned.1.call-start = ((), (), s32[]{:S(2)}) async-start(), calls=%async_computation.15 | async-start | bytes 2654208 | tf_op jit(solution)/shard_map/all_gather | solution.py:220
  664.4 73.1 %all-reduce.5.cloned.1.call-start = ((), (), s32[]{:S(2)}) async-start(), calls=%async_computation.16 | async-start | bytes 1179648 | tf_op jit(solution)/shard_map/psum | solution.py:228
  694.2 74.3 %copy-start.3 = (bf16[2,768,768]{2,1,0:T(8,128)(2,1)S(1)}, bf16[2,768,768]{2,1,0:T(8,128)(2,1)}, u32[]{:S(2)}) copy-start(bf16[2,768,768]{2,1,0:T(8,128)(2,1)} %all-gather.42.cloned.1.call-done) | copy-start | bytes 7077892
  697.8 70.7 %all-gather.44.cloned.1.call-start = ((), (), s32[]{:S(2)}) async-start(), calls=%async_computation.17 | async-start | bytes 2654208 | tf_op jit(solution)/shard_map/all_gather | solution.py:233
  739.4 55.3 %all-gather.54.cloned.1.call-start = ((), (), s32[]{:S(2)}) async-start(), calls=%async_computation.24 | async-start | bytes 1327104 | tf_op jit(solution)/shard_map/all_gather | solution.py:219
  742.5 83.7 %all-gather.46.cloned.1.call-start = ((), (), s32[]{:S(2)}) async-start(), calls=%async_computation.18 | async-start | bytes 2654208 | tf_op jit(solution)/shard_map/all_gather | solution.py:220
  772.5 79.3 %all-gather.32.cloned.1.call-start = ((), (), s32[]{:S(2)}) async-start(), calls=%async_computation.10 | async-start | bytes 1327104 | tf_op jit(solution)/shard_map/all_gather | solution.py:232
  797.3 54.5 %copy-start.7 = (f32[1,96,768]{2,1,0:T(8,128)S(1)}, f32[1,96,768]{2,1,0:T(8,128)}, u32[]{:S(2)}) copy-start(f32[1,96,768]{2,1,0:T(8,128)} %get-tuple-element.33) | copy-start | bytes 884740
  797.3 54.5 %copy-start.19 = (bf16[96,768]{1,0:T(8,128)(2,1)S(1)}, bf16[96,768]{1,0:T(8,128)(2,1)}, u32[]{:S(2)}) copy-start(bf16[96,768]{1,0:T(8,128)(2,1)} %get-tuple-element.61) | copy-start | bytes 442372
  797.3 96.4 %all-reduce.7.cloned.1.call-start = ((), (), s32[]{:S(2)}) async-start(), calls=%async_computation.19 | async-start | bytes 1179648 | tf_op jit(solution)/shard_map/psum | solution.py:228
  829.4 89.4 %all-gather.34.cloned.1.call-start = ((), (), s32[]{:S(2)}) async-start(), calls=%async_computation.11 | async-start | bytes 1327104 | tf_op jit(solution)/shard_map/all_gather | solution.py:219
  854.4 95.1 %copy-start.2 = (bf16[2,768,768]{2,1,0:T(8,128)(2,1)S(1)}, bf16[2,768,768]{2,1,0:T(8,128)(2,1)}, u32[]{:S(2)}) copy-start(bf16[2,768,768]{2,1,0:T(8,128)(2,1)} %all-gather.46.cloned.1.call-done) | copy-start | bytes 7077892
  854.5 95.0 %all-gather.48.cloned.1.call-start = ((), (), s32[]{:S(2)}) async-start(), calls=%async_computation.20 | async-start | bytes 2654208 | tf_op jit(solution)/shard_map/all_gather | solution.py:233
  895.5 79.7 %all-gather.36.cloned.1.call-start = ((), (), s32[]{:S(2)}) async-start(), calls=%async_computation.12 | async-start | bytes 1327104 | tf_op jit(solution)/shard_map/all_gather | solution.py:232
  921.5 84.5 %all-gather.50.cloned.1.call-start = ((), (), s32[]{:S(2)}) async-start(), calls=%async_computation.21 | async-start | bytes 2654208 | tf_op jit(solution)/shard_map/all_gather | solution.py:220
  953.5 78.2 %all-gather.38.cloned.1.call-start = ((), (), s32[]{:S(2)}) async-start(), calls=%async_computation.13 | async-start | bytes 1327104 | tf_op jit(solution)/shard_map/all_gather | solution.py:219
  978.4 95.3 %all-reduce.9.cloned.1.call-start = ((), (), s32[]{:S(2)}) async-start(), calls=%async_computation.22 | async-start | bytes 1179648 | tf_op jit(solution)/shard_map/psum | solution.py:228
  1009.4 66.2 %copy-start.59 = (f32[128]{0:T(128)S(1)}, f32[128]{0:T(128)}, u32[]{:S(2)}) copy-start(f32[128]{0:T(128)} %get-tuple-element.14) | copy-start | bytes 1540
  1009.4 66.2 %copy-start.58 = (f32[128]{0:T(128)S(1)}, f32[128]{0:T(128)}, u32[]{:S(2)}) copy-start(f32[128]{0:T(128)} %get-tuple-element.15) | copy-start | bytes 1540
  1009.4 66.3 %copy-start.33 = (f32[128,768]{1,0:T(8,128)S(1)}, f32[128,768]{1,0:T(8,128)}, u32[]{:S(2)}) copy-start(f32[128,768]{1,0:T(8,128)} %get-tuple-element.60) | copy-start | bytes 1179652
  1009.4 66.3 %copy-start.53 = (f32[128]{0:T(128)S(1)}, f32[128]{0:T(128)}, u32[]{:S(2)}) copy-start(f32[128]{0:T(128)} %copy-done.51) | copy-start | bytes 1540
  1009.4 67.2 %copy-start.22 = (bf16[128,3072]{1,0:T(8,128)(2,1)S(1)}, bf16[128,3072]{1,0:T(8,128)(2,1)}, u32[]{:S(2)}) copy-start(bf16[128,3072]{1,0:T(8,128)(2,1)} %get-tuple-element.52) | copy-start | bytes 2359300
  1009.4 67.2 %copy-start.48 = (f32[768]{0:T(1024)S(1)}, f32[768]{0:T(1024)}, u32[]{:S(2)}) copy-start(f32[768]{0:T(1024)} %get-tuple-element.19) | copy-start | bytes 9220
  1009.4 89.6 %all-gather.40.cloned.1.call-start = ((), (), s32[]{:S(2)}) async-start(), calls=%async_computation.14 | async-start | bytes 1327104 | tf_op jit(solution)/shard_map/all_gather | solution.py:232
  1034.2 95.6 %all-gather.52.cloned.1.call-start = ((), (), s32[]{:S(2)}) async-start(), calls=%async_computation.23 | async-start | bytes 2654208 | tf_op jit(solution)/shard_map/all_gather | solution.py:233
  (36 other events, 697.6 us)
Sparse Core Ops, SparseCore 0:
  10.4 26.6 all-gather.19
  39.6 28.8 all-gather.23
  70.1 89.3 all-gather.21
  160.9 165.1 all-gather.25
  330.8 85.3 all-gather.29
  417.6 102.2 all-gather.27
  523.3 40.7 reduce-scatter.2
  567.5 53.7 reduce-scatter.4
  664.6 29.5 all-gather.41
  697.9 39.6 all-reduce.4
  740.1 28.3 all-gather.43
  770.8 23.9 all-gather.53
  797.2 28.8 all-gather.45
  827.8 23.9 all-gather.31
  854.0 39.6 all-reduce.6
  895.4 23.3 all-gather.33
  920.6 28.8 all-gather.47
  951.2 23.9 all-gather.35
  977.1 28.8 all-gather.49
  1007.7 23.9 all-gather.37
  1034.0 39.6 all-reduce.8
  1075.6 23.3 all-gather.39
  1100.9 28.8 all-gather.51
where the time goes:
time: 1140 us
  waiting for transfers between devices  766 us (67%)
  blocking collectives  242 us (21%)
  matrix products  83.9 us (7%)
  other arithmetic  25.5 us (2%)
  between operations  15.5 us (1%)
    all_gather x1, waiting for transfers between devices, on_device(): lax.all_gather(ffn_rows, 'group', axis=2, tiled=True)  158 us
    psum x3, waiting for transfers between devices, orthogonalize_rows(): ffn_gram = lax.psum(ffn_part, 'group')  118 us
    all_gather x1, waiting for transfers between devices, on_device(): lax.all_gather(attn_rows, 'group', axis=0, tiled=True)  89.4 us
    all_gather x3, waiting for transfers between devices, orthogonalize_rows(): lax.all_gather(ffn_iter_b, 'dp', axis=1, tiled=True)  86 us
    all_gather x3, waiting for transfers between devices, orthogonalize_rows(): lax.all_gather(ffn_gram_b, 'dp', axis=1, tiled=True)  81.6 us
    all_gather x3, waiting for transfers between devices, orthogonalize_rows(): lax.all_gather(attn_iter_b, 'dp', axis=0, tiled=True)  67.7 us
    all_gather x3, waiting for transfers between devices, orthogonalize_rows(): lax.all_gather(attn_gram_b, 'dp', axis=0, tiled=True)  60.1 us
    reduce_scatter x1, waiting for transfers between devices, on_device(): lax.psum_scatter(ffn_term, 'dp', scatter_dimension=1, tiled=True)  46.3 us
  transfers between devices with their start and end apart: 23, of which 20 were waited for; matrix products, arithmetic and copies ran while one was open for 8% of the time, Pallas kernels for 0%

commit v1 on v0

--- a/solution.py
+++ b/solution.py
@@ -12,6 +12,19 @@
 momentum_rate = 0.9
 muon_rate = 0.8
 vector_rate = 0.1
+
+
+def gather_around(x, axis, dim):
+    size, place, rows = (lax.axis_size(axis), lax.axis_index(axis), x.shape[dim])
+    forward = [(i, (i + 1) % size) for i in range(size)]
+    result = jnp.zeros((*x.shape[:dim], size * rows, *x.shape[dim + 1 :]), x.dtype)
+    carried = x
+    for step in range(size):
+        holder = (place - step) % size
+        result = lax.dynamic_update_slice_in_dim(result, carried, holder * rows, axis=dim)
+        if step < size - 1:
+            carried = lax.ppermute(carried, axis, forward)
+    return result
 
 
 def norm_forward(rows):
@@ -268,7 +281,7 @@
         lax.all_gather(own_ffn, "dp", axis=1, tiled=True),
     )
     attn_whole, ffn_whole = (
-        lax.all_gather(attn_rows, "group", axis=0, tiled=True),
+        gather_around(attn_rows, "group", 0),
         lax.all_gather(ffn_rows, "group", axis=2, tiled=True),
     )
     outputs, input_grad, vector_terms, pieces = layer_block(

time: 1140 us -> 1120 us (0.982)
  waiting for transfers between devices: 766 us -> 692 us
  starting transfers between devices: 1.17 us -> 50.5 us
    ppermute x0 -> x3, waiting for transfers between devices: none -> 141 us  [gather_around(): carried = lax.ppermute(carried, axis, forward)]
    all_gather x1, waiting for transfers between devices: 158 us -> 30.1 us  [on_device(): lax.all_gather(ffn_rows, 'group', axis=2, tiled=True)]
    all_gather x1 -> x0, waiting for transfers between devices: 89.4 us -> none  [on_device(): lax.all_gather(attn_rows, 'group', axis=0, tiled=True)]
    ppermute x0 -> x3, starting transfers between devices: none -> 49.3 us  [gather_around(): carried = lax.ppermute(carried, axis, forward)]
  transfers between devices with their start and end apart: 23 -> 25, of which waited for: 20 -> 22; matrix products, arithmetic and copies ran while one was open for 8% -> 8% of each run, Pallas kernels for 0% -> 0%
where the time goes in v1:
time: 1120 us
  waiting for transfers between devices  692 us (62%)
  blocking collectives  243 us (22%)
  matrix products  82.5 us (7%)
  starting transfers between devices  50.5 us (5%)
  other arithmetic  25.5 us (2%)
  between operations  15.8 us (1%)
    ppermute x3, waiting for transfers between devices, gather_around(): carried = lax.ppermute(carried, axis, forward)  141 us
    psum x3, waiting for transfers between devices, orthogonalize_rows(): ffn_gram = lax.psum(ffn_part, 'group')  118 us
    all_gather x3, waiting for transfers between devices, orthogonalize_rows(): lax.all_gather(ffn_iter_b, 'dp', axis=1, tiled=True)  85.7 us
    all_gather x3, waiting for transfers between devices, orthogonalize_rows(): lax.all_gather(ffn_gram_b, 'dp', axis=1, tiled=True)  81.4 us
    all_gather x3, waiting for transfers between devices, orthogonalize_rows(): lax.all_gather(attn_iter_b, 'dp', axis=0, tiled=True)  68 us
    all_gather x3, waiting for transfers between devices, orthogonalize_rows(): lax.all_gather(attn_gram_b, 'dp', axis=0, tiled=True)  60.2 us
    ppermute x3, starting transfers between devices, gather_around(): carried = lax.ppermute(carried, axis, forward)  49.3 us
    reduce_scatter x1, waiting for transfers between devices, on_device(): lax.psum_scatter(ffn_term, 'dp', scatter_dimension=1, tiled=True)  48.9 us
  transfers between devices with their start and end apart: 25, of which 22 were waited for; matrix products, arithmetic and copies ran while one was open for 8% of the time, Pallas kernels for 0%

profile of v1, /device:TPU:0, one launch (start us, length us, event | category | flops | bytes accessed | tf_op | source)
XLA Modules:
  0.0 1120.3 jit_solution(14885148961381147243)
XLA Ops:
  10.9 31.2 %all-gather.21.cloned.1.call-done = bf16[2,768,768]{2,1,0:T(8,128)(2,1)} async-done(((bf16[2,96,768]{2,1,0:T(8,128)(2,1)}), bf16[2,768,768]{2,1,0:T(8,128)(2,1)}) %all-gather.21.cloned.1.call-update) | async-done | bytes 2359312 | tf_op jit(solution)/shard_map/all_gather | solution.py:281
  42.2 26.3 %all-gather.19.cloned.1.call-done = bf16[1,768,768]{2,1,0:T(8,128)(2,1)} async-done(((bf16[1,96,768]{2,1,0:T(8,128)(2,1)}), bf16[1,768,768]{2,1,0:T(8,128)(2,1)}) %all-gather.19.cloned.1.call-update) | async-done | bytes 1179664 | tf_op jit(solution)/shard_map/all_gather | solution.py:280
  70.0 43.6 %collective-permute-done = bf16[1,768,768]{2,1,0:T(8,128)(2,1)S(1)} collective-permute-done((bf16[1,768,768]{2,1,0:T(8,128)(2,1)}, bf16[1,768,768]{2,1,0:T(8,128)(2,1)S(1)}, u32[]{:S(2)}, u32[]{:S(2)}) %collective-permute-start) | collective-permute-done | bytes 1179680 | tf_op jit(solution)/shard_map/ppermute | solution.py:26
  113.7 18.1 %collective-permute-start.1 = (bf16[1,768,768]{2,1,0:T(8,128)(2,1)S(1)}, bf16[1,768,768]{2,1,0:T(8,128)(2,1)S(1)}, u32[]{:S(2)}, u32[]{:S(2)}) collective-permute-start(bf16[1,768,768]{2,1,0:T(8,128)(2,1)S(1)} %collective-permute-done), channel_id=1, source_target_pairs={{0,1},{1,2},{2,3},{3,0},{4,5},{5,6},{6,7},{7,4},{8,9},{9,10},{10,1... | collective-permute-start | bytes 3538952 | tf_op jit(solution)/shard_map/ppermute | solution.py:26
  132.9 48.5 %collective-permute-done.1 = bf16[1,768,768]{2,1,0:T(8,128)(2,1)S(1)} collective-permute-done((bf16[1,768,768]{2,1,0:T(8,128)(2,1)S(1)}, bf16[1,768,768]{2,1,0:T(8,128)(2,1)S(1)}, u32[]{:S(2)}, u32[]{:S(2)}) %collective-permute-start.1) | collective-permute-done | bytes 1179680 | tf_op jit(solution)/shard_map/ppermute | solution.py:26
  181.4 29.8 %collective-permute-start.2 = (bf16[1,768,768]{2,1,0:T(8,128)(2,1)S(1)}, bf16[1,768,768]{2,1,0:T(8,128)(2,1)S(1)}, u32[]{:S(2)}, u32[]{:S(2)}) collective-permute-start(bf16[1,768,768]{2,1,0:T(8,128)(2,1)S(1)} %collective-permute-done.1), channel_id=1, source_target_pairs={{0,1},{1,2},{2,3},{3,0},{4,5},{5,6},{6,7},{7,4},{8,9},{9,10},{10,1... | collective-permute-start | bytes 3538952 | tf_op jit(solution)/shard_map/ppermute | solution.py:26
  213.1 49.1 %collective-permute-done.2 = bf16[1,768,768]{2,1,0:T(8,128)(2,1)S(1)} collective-permute-done((bf16[1,768,768]{2,1,0:T(8,128)(2,1)S(1)}, bf16[1,768,768]{2,1,0:T(8,128)(2,1)S(1)}, u32[]{:S(2)}, u32[]{:S(2)}) %collective-permute-start.2) | collective-permute-done | bytes 1179680 | tf_op jit(solution)/shard_map/ppermute | solution.py:26
  271.4 30.1 %all-gather.23.cloned.1.call-done = bf16[2,768,3072]{2,1,0:T(8,128)(2,1)} async-done(((bf16[2,768,768]{2,1,0:T(8,128)(2,1)}), bf16[2,768,3072]{2,1,0:T(8,128)(2,1)}) %all-gather.23.cloned.1.call-update) | async-done | bytes 9437200 | tf_op jit(solution)/shard_map/all_gather | solution.py:285
  301.5 4.6 maximum_convert_fusion
  306.8 5.2 fusion.93
  312.1 30.6 %all_gather.79 = bf16[512,768]{1,0:T(8,128)(2,1)} all-gather(bf16[128,768]{1,0:T(8,128)(2,1)S(1)} %add_convert_fusion.1), channel_id=1, replica_groups=mesh['dp'=8,'group'=4] {'group'}, dimensions={0}, use_global_device_ids=true | all-gather | bytes 983040 | tf_op jit(solution)/shard_map/all_gather | solution.py:187
  342.9 28.2 %all_gather.78 = bf16[512,768]{1,0:T(8,128)(2,1)} all-gather(bf16[128,768]{1,0:T(8,128)(2,1)S(1)} %copy.58), channel_id=1, replica_groups=mesh['dp'=8,'group'=4] {'group'}, dimensions={0}, use_global_device_ids=true | all-gather | bytes 983040 | tf_op jit(solution)/shard_map/all_gather | solution.py:188
  371.1 5.0 multiply_reduce_fusion.2
  386.0 21.3 %all_gather.83 = bf16[512,768]{1,0:T(8,128)(2,1)S(1)} all-gather(bf16[128,768]{1,0:T(8,128)(2,1)} %copy-done.34), channel_id=1, replica_groups=mesh['dp'=8,'group'=4] {'group'}, dimensions={0}, use_global_device_ids=true | all-gather | bytes 983040 | tf_op jit(solution)/shard_map/all_gather | solution.py:192
  407.3 28.9 %all_gather.80 = bf16[512,768]{1,0:T(8,128)(2,1)S(1)} all-gather(bf16[128,768]{1,0:T(8,128)(2,1)S(1)} %copy-done.28), channel_id=1, replica_groups=mesh['dp'=8,'group'=4] {'group'}, dimensions={0}, use_global_device_ids=true | all-gather | bytes 983040 | tf_op jit(solution)/shard_map/all_gather | solution.py:189
  436.2 29.1 %all_gather.81 = bf16[512,768]{1,0:T(8,128)(2,1)S(1)} all-gather(bf16[128,768]{1,0:T(8,128)(2,1)} %copy.60), channel_id=1, replica_groups=mesh['dp'=8,'group'=4] {'group'}, dimensions={0}, use_global_device_ids=true | all-gather | bytes 983040 | tf_op jit(solution)/shard_map/all_gather | solution.py:190
  465.3 28.5 %all_gather.82 = bf16[512,768]{1,0:T(8,128)(2,1)S(1)} all-gather(bf16[128,768]{1,0:T(8,128)(2,1)S(1)} %copy-done.29), channel_id=1, replica_groups=mesh['dp'=8,'group'=4] {'group'}, dimensions={0}, use_global_device_ids=true | all-gather | bytes 983040 | tf_op jit(solution)/shard_map/all_gather | solution.py:191
  497.2 19.9 %all_gather.87 = bf16[512,768]{1,0:T(8,128)(2,1)} all-gather(bf16[128,768]{1,0:T(8,128)(2,1)S(1)} %copy-done.33), channel_id=1, replica_groups=mesh['dp'=8,'group'=4] {'group'}, dimensions={0}, use_global_device_ids=true | all-gather | bytes 983040 | tf_op jit(solution)/shard_map/all_gather | solution.py:194
  517.1 16.6 %all_gather.84 = bf16[512,768]{1,0:T(8,128)(2,1)} all-gather(bf16[128,768]{1,0:T(8,128)(2,1)S(1)} %copy-done.31), channel_id=1, replica_groups=mesh['dp'=8,'group'=4] {'group'}, dimensions={0}, use_global_device_ids=true | all-gather | bytes 983040 | tf_op jit(solution)/shard_map/all_gather | solution.py:193
  545.4 3.2 multiply_reduce_fusion.3
  552.0 48.9 %reduce-scatter.5.cloned.1.call-done = f32[2,96,768]{2,1,0:T(8,128)} async-done(((f32[2,768,768]{2,1,0:T(8,128)}), f32[2,96,768]{2,1,0:T(8,128)}) %reduce-scatter.5.cloned.1.call-update) | async-done | bytes 589840 | tf_op jit(solution)/shard_map/reduce_scatter | solution.py:293
  603.0 40.2 %all-reduce = (f32[12,768]{1,0:T(8,128)}, f32[6]{0:T(128)S(1)}) all-reduce(f32[12,768]{1,0:T(8,128)S(1)} %concatenate.6, f32[6]{0:T(128)S(1)} %pad_maximum_fusion.1), channel_id=1, replica_groups=mesh['dp'=8,'group'=4] {'dp','group'}, use_global_device_ids=true, to_apply=%region_24.25 | all-reduce | flops 9222 | bytes 73776 | tf_op jit(solution)/shard_map/psum | solution.py:307
  644.2 29.7 %all-gather.39.cloned.1.call-done = bf16[2,768,768]{2,1,0:T(8,128)(2,1)} async-done(((bf16[2,96,768]{2,1,0:T(8,128)(2,1)}), bf16[2,768,768]{2,1,0:T(8,128)(2,1)}) %all-gather.39.cloned.1.call-update) | async-done | bytes 2359312 | tf_op jit(solution)/shard_map/all_gather | solution.py:233
  673.9 3.6 fusion.112
  677.5 39.8 %all-reduce.5.cloned.1.call-done = f32[2,96,768]{2,1,0:T(8,128)} async-done(((f32[2,96,768]{2,1,0:T(8,128)}), f32[2,96,768]{2,1,0:T(8,128)}) %all-reduce.5.cloned.1.call-update) | async-done | bytes 589840 | tf_op jit(solution)/shard_map/psum | solution.py:241
  722.2 25.8 %all-gather.41.cloned.1.call-done = bf16[2,768,768]{2,1,0:T(8,128)(2,1)} async-done(((bf16[2,96,768]{2,1,0:T(8,128)(2,1)}), bf16[2,768,768]{2,1,0:T(8,128)(2,1)}) %all-gather.41.cloned.1.call-update) | async-done | bytes 2359312 | tf_op jit(solution)/shard_map/all_gather | solution.py:246
  748.0 4.0 fusion.104
  752.0 22.4 %all-gather.51.cloned.1.call-done = bf16[1,768,768]{2,1,0:T(8,128)(2,1)} async-done(((bf16[1,96,768]{2,1,0:T(8,128)(2,1)}), bf16[1,768,768]{2,1,0:T(8,128)(2,1)}) %all-gather.51.cloned.1.call-update) | async-done | bytes 1179664 | tf_op jit(solution)/shard_map/all_gather | solution.py:232
  777.0 28.6 %all-gather.43.cloned.1.call-done = bf16[2,768,768]{2,1,0:T(8,128)(2,1)} async-done(((bf16[2,96,768]{2,1,0:T(8,128)(2,1)}), bf16[2,768,768]{2,1,0:T(8,128)(2,1)}) %all-gather.43.cloned.1.call-update) | async-done | bytes 2359312 | tf_op jit(solution)/shard_map/all_gather | solution.py:233
  805.6 3.3 fusion.113
  809.0 22.4 %all-gather.29.cloned.1.call-done = bf16[768,768]{1,0:T(8,128)(2,1)} async-done(((bf16[96,768]{1,0:T(8,128)(2,1)}), bf16[768,768]{1,0:T(8,128)(2,1)}) %all-gather.29.cloned.1.call-update) | async-done | bytes 1179664 | tf_op jit(solution)/shard_map/all_gather | solution.py:245
  831.5 2.6 fusion.100
  834.2 39.2 %all-reduce.7.cloned.1.call-done = f32[2,96,768]{2,1,0:T(8,128)} async-done(((f32[2,96,768]{2,1,0:T(8,128)}), f32[2,96,768]{2,1,0:T(8,128)}) %all-reduce.7.cloned.1.call-update) | async-done | bytes 589840 | tf_op jit(solution)/shard_map/psum | solution.py:241
  875.2 23.3 %all-gather.31.cloned.1.call-done = bf16[768,768]{1,0:T(8,128)(2,1)} async-done(((bf16[96,768]{1,0:T(8,128)(2,1)}), bf16[768,768]{1,0:T(8,128)(2,1)}) %all-gather.31.cloned.1.call-update) | async-done | bytes 1179664 | tf_op jit(solution)/shard_map/all_gather | solution.py:232
  898.5 2.6 fusion.101
  901.2 28.0 %all-gather.45.cloned.1.call-done = bf16[2,768,768]{2,1,0:T(8,128)(2,1)} async-done(((bf16[2,96,768]{2,1,0:T(8,128)(2,1)}), bf16[2,768,768]{2,1,0:T(8,128)(2,1)}) %all-gather.45.cloned.1.call-update) | async-done | bytes 2359312 | tf_op jit(solution)/shard_map/all_gather | solution.py:246
  929.2 4.0 fusion.105
  933.3 21.6 %all-gather.33.cloned.1.call-done = bf16[768,768]{1,0:T(8,128)(2,1)} async-done(((bf16[96,768]{1,0:T(8,128)(2,1)}), bf16[768,768]{1,0:T(8,128)(2,1)}) %all-gather.33.cloned.1.call-update) | async-done | bytes 1179664 | tf_op jit(solution)/shard_map/all_gather | solution.py:245
  954.9 3.2 fusion.102
  958.1 27.4 %all-gather.47.cloned.1.call-done = bf16[2,768,768]{2,1,0:T(8,128)(2,1)} async-done(((bf16[2,96,768]{2,1,0:T(8,128)(2,1)}), bf16[2,768,768]{2,1,0:T(8,128)(2,1)}) %all-gather.47.cloned.1.call-update) | async-done | bytes 2359312 | tf_op jit(solution)/shard_map/all_gather | solution.py:233
  985.6 3.3 fusion.114
  989.0 22.4 %all-gather.35.cloned.1.call-done = bf16[768,768]{1,0:T(8,128)(2,1)} async-done(((bf16[96,768]{1,0:T(8,128)(2,1)}), bf16[768,768]{1,0:T(8,128)(2,1)}) %all-gather.35.cloned.1.call-update) | async-done | bytes 1179664 | tf_op jit(solution)/shard_map/all_gather | solution.py:232
  1014.2 39.0 %all-reduce.9.cloned.1.call-done = f32[2,96,768]{2,1,0:T(8,128)} async-done(((f32[2,96,768]{2,1,0:T(8,128)}), f32[2,96,768]{2,1,0:T(8,128)}) %all-reduce.9.cloned.1.call-update) | async-done | bytes 589840 | tf_op jit(solution)/shard_map/psum | solution.py:241
  1056.1 4.8 fusion.19
  1062.4 16.2 %all-gather.37.cloned.1.call-done = bf16[768,768]{1,0:T(8,128)(2,1)} async-done(((bf16[96,768]{1,0:T(8,128)(2,1)}), bf16[768,768]{1,0:T(8,128)(2,1)}) %all-gather.37.cloned.1.call-update) | async-done | bytes 1179664 | tf_op jit(solution)/shard_map/all_gather | solution.py:245
  1078.6 3.2 fusion.34
  1081.8 27.6 %all-gather.49.cloned.1.call-done = bf16[2,768,768]{2,1,0:T(8,128)(2,1)} async-done(((bf16[2,96,768]{2,1,0:T(8,128)(2,1)}), bf16[2,768,768]{2,1,0:T(8,128)(2,1)}) %all-gather.49.cloned.1.call-update) | async-done | bytes 2359312 | tf_op jit(solution)/shard_map/all_gather | solution.py:246
  1109.4 4.0 fusion.7
  (256 shorter events, 65.5 us)
Async XLA Ops:
  7.2 124.6 %copy-start.59 = (s32[1,4]{1,0:T(1,128)S(1)}, s32[1,4]{1,0:T(1,128)}, u32[]{:S(2)}) copy-start(s32[1,4]{1,0:T(1,128)} %param.11) | copy-start | bytes 52
  7.2 124.8 %slice-start = ((f32[12,768]{1,0:T(8,128)}), f32[4,768]{1,0:T(4,128)S(1)}, s32[]{:S(2)}) async-start(f32[12,768]{1,0:T(8,128)} %param.16), calls=%async_computation.24 | async-start | bytes 24576 | tf_op jit(solution)/shard_map/slice | solution.py:58
  7.2 124.9 %copy-start.38 = (f32[12,768]{1,0:T(8,128)S(1)}, f32[12,768]{1,0:T(8,128)}, u32[]{:S(2)}) copy-start(f32[12,768]{1,0:T(8,128)} %param.16) | copy-start | bytes 110596
  7.2 124.7 %copy-start.1 = (f32[128,768]{1,0:T(8,128)S(1)}, f32[128,768]{1,0:T(8,128)}, u32[]{:S(2)}) copy-start(f32[128,768]{1,0:T(8,128)} %param.9) | copy-start | bytes 1179652
  7.2 34.9 %all-gather.21.cloned.1.call-start = ((), (), s32[]{:S(2)}) async-start(), calls=%async_computation.3 | async-start | bytes 2654208 | tf_op jit(solution)/shard_map/all_gather | solution.py:281
  9.2 59.4 %all-gather.19.cloned.1.call-start = ((), (), s32[]{:S(2)}) async-start(), calls=%async_computation.2 | async-start | bytes 1327104 | tf_op jit(solution)/shard_map/all_gather | solution.py:280
  10.9 290.7 %all-gather.23.cloned.1.call-start = ((), (), s32[]{:S(2)}) async-start(), calls=%async_computation.4 | async-start | bytes 11796480 | tf_op jit(solution)/shard_map/all_gather | solution.py:285
  42.2 491.6 %all-gather.27.cloned.1.call-start = ((), (), s32[]{:S(2)}) async-start(), calls=%async_computation.7 | async-start | bytes 3932160 | tf_op jit(solution)/shard_map/all_gather | solution.py:196
  68.5 45.1 %collective-permute-start = (bf16[1,768,768]{2,1,0:T(8,128)(2,1)}, bf16[1,768,768]{2,1,0:T(8,128)(2,1)S(1)}, u32[]{:S(2)}, u32[]{:S(2)}) collective-permute-start(bf16[1,768,768]{2,1,0:T(8,128)(2,1)} %all-gather.19.cloned.1.call-done), channel_id=1, source_target_pairs={{0,1},{1,2},{2,3},{3,0},{4,5},{5,6},{6,7},{7,4},{8,9},{9,10},{10,1... | collective-permute-start | bytes 3538952 | tf_op jit(solution)/shard_map/ppermute | solution.py:26
  113.7 67.7 %collective-permute-start.1 = (bf16[1,768,768]{2,1,0:T(8,128)(2,1)S(1)}, bf16[1,768,768]{2,1,0:T(8,128)(2,1)S(1)}, u32[]{:S(2)}, u32[]{:S(2)}) collective-permute-start(bf16[1,768,768]{2,1,0:T(8,128)(2,1)S(1)} %collective-permute-done), channel_id=1, source_target_pairs={{0,1},{1,2},{2,3},{3,0},{4,5},{5,6},{6,7},{7,4},{8,9},{9,10},{10,1... | collective-permute-start | bytes 3538952 | tf_op jit(solution)/shard_map/ppermute | solution.py:26
  132.7 79.1 %copy-start.47 = (f32[128]{0:T(128)}, f32[128]{0:T(128)S(1)}, u32[]{:S(2)}) copy-start(f32[128]{0:T(128)S(1)} %broadcast_multiply_fusion.7) | copy-start | bytes 1540
  181.4 80.8 %collective-permute-start.2 = (bf16[1,768,768]{2,1,0:T(8,128)(2,1)S(1)}, bf16[1,768,768]{2,1,0:T(8,128)(2,1)S(1)}, u32[]{:S(2)}, u32[]{:S(2)}) collective-permute-start(bf16[1,768,768]{2,1,0:T(8,128)(2,1)S(1)} %collective-permute-done.1), channel_id=1, source_target_pairs={{0,1},{1,2},{2,3},{3,0},{4,5},{5,6},{6,7},{7,4},{8,9},{9,10},{10,1... | collective-permute-start | bytes 3538952 | tf_op jit(solution)/shard_map/ppermute | solution.py:26
  271.1 100.0 %copy-start.52 = (f32[128]{0:T(128)}, f32[128]{0:T(128)S(1)}, u32[]{:S(2)}) copy-start(f32[128]{0:T(128)S(1)} %broadcast_multiply_fusion.6) | copy-start | bytes 1540
  271.3 99.8 %copy-start.56 = (f32[128]{0:T(128)}, f32[128]{0:T(128)S(1)}, u32[]{:S(2)}) copy-start(f32[128]{0:T(128)S(1)} %add_rsqrt_fusion) | copy-start | bytes 1540
  306.1 229.8 %all-gather.25.cloned.1.call-start = ((), (), s32[]{:S(2)}) async-start(), calls=%async_computation.6 | async-start | bytes 3932160 | tf_op jit(solution)/shard_map/all_gather | solution.py:195
  312.0 236.9 %reduce-scatter.3.cloned.1.call-start = ((), (), s32[]{:S(2)}) async-start(), calls=%async_computation.5 | async-start | bytes 2654208 | tf_op jit(solution)/shard_map/reduce_scatter | solution.py:292
  383.2 82.1 %copy-start.15 = (bf16[12,64,128]{2,1,0:T(8,128)(2,1)}, bf16[12,64,128]{2,1,0:T(8,128)(2,1)S(1)}, u32[]{:S(2)}) copy-start(bf16[12,64,128]{2,1,0:T(8,128)(2,1)S(1)} %convolution_convert_fusion) | copy-start | bytes 589828
  385.1 111.1 %copy-start.11 = (bf16[128,12,64]{0,2,1:T(8,128)(2,1)}, bf16[128,12,64]{0,2,1:T(8,128)(2,1)S(1)}, u32[]{:S(2)}) copy-start(bf16[128,12,64]{0,2,1:T(8,128)(2,1)S(1)} %get-tuple-element.45) | copy-start | bytes 589828
  385.1 108.6 %copy-start.26 = (bf16[512,768]{1,0:T(8,128)(2,1)S(1)}, bf16[512,768]{1,0:T(8,128)(2,1)}, u32[]{:S(2)}) copy-start(bf16[512,768]{1,0:T(8,128)(2,1)} %all_gather.79) | copy-start | bytes 2359300
  385.1 108.6 %copy-start.27 = (bf16[512,768]{1,0:T(8,128)(2,1)S(1)}, bf16[512,768]{1,0:T(8,128)(2,1)}, u32[]{:S(2)}) copy-start(bf16[512,768]{1,0:T(8,128)(2,1)} %all_gather.78) | copy-start | bytes 2359300
  386.0 79.3 %copy-start.29 = (bf16[128,768]{1,0:T(8,128)(2,1)S(1)}, bf16[128,768]{1,0:T(8,128)(2,1)}, u32[]{:S(2)}) copy-start(bf16[128,768]{1,0:T(8,128)(2,1)} %copy.61) | copy-start | bytes 589828
  496.3 104.6 %reduce-scatter.5.cloned.1.call-start = ((), (), s32[]{:S(2)}) async-start(), calls=%async_computation.8 | async-start | bytes 5308416 | tf_op jit(solution)/shard_map/reduce_scatter | solution.py:293
  540.7 133.2 %all-gather.39.cloned.1.call-start = ((), (), s32[]{:S(2)}) async-start(), calls=%async_computation.14 | async-start | bytes 2654208 | tf_op jit(solution)/shard_map/all_gather | solution.py:233
  545.3 55.6 %copy-start.35 = (f32[2,96,768]{2,1,0:T(8,128)S(1)}, f32[2,96,768]{2,1,0:T(8,128)}, u32[]{:S(2)}) copy-start(f32[2,96,768]{2,1,0:T(8,128)} %param.15) | copy-start | bytes 1769476
  644.1 73.2 %all-reduce.5.cloned.1.call-start = ((), (), s32[]{:S(2)}) async-start(), calls=%async_computation.15 | async-start | bytes 1179648 | tf_op jit(solution)/shard_map/psum | solution.py:241
  673.9 74.1 %copy-start.4 = (bf16[2,768,768]{2,1,0:T(8,128)(2,1)S(1)}, bf16[2,768,768]{2,1,0:T(8,128)(2,1)}, u32[]{:S(2)}) copy-start(bf16[2,768,768]{2,1,0:T(8,128)(2,1)} %all-gather.39.cloned.1.call-done) | copy-start | bytes 7077892
  677.4 70.5 %all-gather.41.cloned.1.call-start = ((), (), s32[]{:S(2)}) async-start(), calls=%async_computation.16 | async-start | bytes 2654208 | tf_op jit(solution)/shard_map/all_gather | solution.py:246
  719.1 55.3 %all-gather.51.cloned.1.call-start = ((), (), s32[]{:S(2)}) async-start(), calls=%async_computation.23 | async-start | bytes 1327104 | tf_op jit(solution)/shard_map/all_gather | solution.py:232
  722.1 83.5 %all-gather.43.cloned.1.call-start = ((), (), s32[]{:S(2)}) async-start(), calls=%async_computation.17 | async-start | bytes 2654208 | tf_op jit(solution)/shard_map/all_gather | solution.py:233
  752.0 79.5 %all-gather.29.cloned.1.call-start = ((), (), s32[]{:S(2)}) async-start(), calls=%async_computation.9 | async-start | bytes 1327104 | tf_op jit(solution)/shard_map/all_gather | solution.py:245
  776.9 54.5 %copy-start.8 = (f32[1,96,768]{2,1,0:T(8,128)S(1)}, f32[1,96,768]{2,1,0:T(8,128)}, u32[]{:S(2)}) copy-start(f32[1,96,768]{2,1,0:T(8,128)} %get-tuple-element.33) | copy-start | bytes 884740
  776.9 54.5 %copy-start.23 = (bf16[96,768]{1,0:T(8,128)(2,1)S(1)}, bf16[96,768]{1,0:T(8,128)(2,1)}, u32[]{:S(2)}) copy-start(bf16[96,768]{1,0:T(8,128)(2,1)} %get-tuple-element.61) | copy-start | bytes 442372
  776.9 96.4 %all-reduce.7.cloned.1.call-start = ((), (), s32[]{:S(2)}) async-start(), calls=%async_computation.18 | async-start | bytes 1179648 | tf_op jit(solution)/shard_map/psum | solution.py:241
  809.0 89.5 %all-gather.31.cloned.1.call-start = ((), (), s32[]{:S(2)}) async-start(), calls=%async_computation.10 | async-start | bytes 1327104 | tf_op jit(solution)/shard_map/all_gather | solution.py:232
  834.1 95.1 %copy-start.3 = (bf16[2,768,768]{2,1,0:T(8,128)(2,1)S(1)}, bf16[2,768,768]{2,1,0:T(8,128)(2,1)}, u32[]{:S(2)}) copy-start(bf16[2,768,768]{2,1,0:T(8,128)(2,1)} %all-gather.43.cloned.1.call-done) | copy-start | bytes 7077892
  834.1 95.0 %all-gather.45.cloned.1.call-start = ((), (), s32[]{:S(2)}) async-start(), calls=%async_computation.19 | async-start | bytes 2654208 | tf_op jit(solution)/shard_map/all_gather | solution.py:246
  875.2 79.7 %all-gather.33.cloned.1.call-start = ((), (), s32[]{:S(2)}) async-start(), calls=%async_computation.11 | async-start | bytes 1327104 | tf_op jit(solution)/shard_map/all_gather | solution.py:245
  901.1 84.4 %all-gather.47.cloned.1.call-start = ((), (), s32[]{:S(2)}) async-start(), calls=%async_computation.20 | async-start | bytes 2654208 | tf_op jit(solution)/shard_map/all_gather | solution.py:233
  933.2 78.2 %all-gather.35.cloned.1.call-start = ((), (), s32[]{:S(2)}) async-start(), calls=%async_computation.12 | async-start | bytes 1327104 | tf_op jit(solution)/shard_map/all_gather | solution.py:232
  958.1 95.2 %all-reduce.9.cloned.1.call-start = ((), (), s32[]{:S(2)}) async-start(), calls=%async_computation.21 | async-start | bytes 1179648 | tf_op jit(solution)/shard_map/psum | solution.py:241
  988.9 66.2 %copy-start.58 = (f32[128]{0:T(128)S(1)}, f32[128]{0:T(128)}, u32[]{:S(2)}) copy-start(f32[128]{0:T(128)} %get-tuple-element.14) | copy-start | bytes 1540
  988.9 66.2 %copy-start.57 = (f32[128]{0:T(128)S(1)}, f32[128]{0:T(128)}, u32[]{:S(2)}) copy-start(f32[128]{0:T(128)} %get-tuple-element.15) | copy-start | bytes 1540
  988.9 66.3 %copy-start.19 = (f32[128,768]{1,0:T(8,128)S(1)}, f32[128,768]{1,0:T(8,128)}, u32[]{:S(2)}) copy-start(f32[128,768]{1,0:T(8,128)} %get-tuple-element.60) | copy-start | bytes 1179652
  988.9 66.3 %copy-start.51 = (f32[128]{0:T(128)S(1)}, f32[128]{0:T(128)}, u32[]{:S(2)}) copy-start(f32[128]{0:T(128)} %copy-done.49) | copy-start | bytes 1540
  988.9 67.2 %copy-start.25 = (bf16[128,3072]{1,0:T(8,128)(2,1)S(1)}, bf16[128,3072]{1,0:T(8,128)(2,1)}, u32[]{:S(2)}) copy-start(bf16[128,3072]{1,0:T(8,128)(2,1)} %get-tuple-element.52) | copy-start | bytes 2359300
  989.0 67.2 %copy-start.53 = (f32[768]{0:T(1024)S(1)}, f32[768]{0:T(1024)}, u32[]{:S(2)}) copy-start(f32[768]{0:T(1024)} %get-tuple-element.19) | copy-start | bytes 9220
  989.0 89.7 %all-gather.37.cloned.1.call-start = ((), (), s32[]{:S(2)}) async-start(), calls=%async_computation.13 | async-start | bytes 1327104 | tf_op jit(solution)/shard_map/all_gather | solution.py:245
  1014.0 95.5 %all-gather.49.cloned.1.call-start = ((), (), s32[]{:S(2)}) async-start(), calls=%async_computation.22 | async-start | bytes 2654208 | tf_op jit(solution)/shard_map/all_gather | solution.py:246
  (40 other events, 726.7 us)
Sparse Core Ops, SparseCore 0:
  10.5 31.5 all-gather.20
  44.6 23.9 all-gather.18
  70.1 231.3 all-gather.22
  306.3 92.2 all-gather.26
  399.9 99.3 all-gather.24
  502.6 41.0 reduce-scatter.2
  547.1 53.7 reduce-scatter.4
  644.2 29.6 all-gather.38
  677.6 39.6 all-reduce.4
  719.6 28.3 all-gather.40
  750.4 23.9 all-gather.50
  776.7 28.8 all-gather.42
  807.5 23.9 all-gather.28
  833.7 39.6 all-reduce.6
  875.1 23.3 all-gather.30
  900.2 28.8 all-gather.44
  930.9 23.9 all-gather.32
  956.7 28.8 all-gather.46
  987.5 23.9 all-gather.34
  1013.6 39.6 all-reduce.8
  1055.2 23.3 all-gather.36
  1080.5 28.8 all-gather.48
